TPU v7x, 256 devices: a whole 4x4x8 slice. The times are simulated.
256 devices in a mesh: segment: 8 (over x, core), seq: 32 (over z, y).
Axes of the slice: x: 4, y: 4, z: 8, core: 2. Of those that a mesh axis runs over, the one named last changes fastest.
Arguments:
- latent: bfloat16 [12288, 1536], P('seq'), may hold values from -4 to 4
- stale_kv: bfloat16 [8, 2, 12288, 1536], P('segment', None, 'seq'), may hold values from -3 to 3
- query_weight: bfloat16 [8, 1536, 1536], P('segment', 'seq'), may hold values from -0.15625 to 0.15625
- key_weight: bfloat16 [8, 1536, 1536], P('segment', 'seq'), may hold values from -0.15625 to 0.15625
- value_weight: bfloat16 [8, 1536, 1536], P('segment', 'seq'), may hold values from -0.15625 to 0.15625
- out_weight: bfloat16 [8, 1536, 1536], P('segment', 'seq'), may hold values from -0.3125 to 0.3125
- query_gain: float32 [8, 128], P('segment'), may hold values from 0.5 to 2
- key_gain: float32 [8, 128], P('segment'), may hold values from 0.5 to 2
- tile_mask: int32 [192, 6], P('seq'), may hold values from -1 to 191, as said below
Outputs:
- section_out: bfloat16 [8, 12288, 1536], P('segment', 'seq')
Inputs may be any that keep to these rules, and one draw needn't show every extreme that they name: `tile_mask`: row g lists the key tiles of query tile g: slot 0 holds g itself, the next slots distinct other tiles whose tile-frame (tile number // 6) differs from that of g by at most one, and the remaining slots -1. Every row lists two or more tiles, and some row lists 6.
All inputs are finite; a program needn't handle non-finite values.
Results may differ from a plain program's by a relative error of at most 0.027.
Values may be sent and summed in bfloat16 or wider, within the bound.
No kernel may reach another device: no remote copies, remote signals or barrier semaphores. Data moves between devices by JAX's collectives and lax.ppermute only.
A program may use at most 128 MiB of HBM per device.

v0:
```python
import math
import jax
import jax.numpy as jnp
from jax import lax
from jax.sharding import PartitionSpec as P

D = 1536
HEADS = 12
HEAD = 128
TILE = 64
PATCHES = 3
TPP = 2
epsilon = 1e-06


def extended(cells, sides, width):
    for axis, dim in sides:
        count = lax.axis_size(axis)
        ends = count - 1
        head = lax.slice_in_dim(cells, 0, width, axis=dim)
        tail = lax.slice_in_dim(cells, cells.shape[dim] - width, cells.shape[dim], axis=dim)
        cells = jnp.concatenate(
            [
                lax.ppermute(tail, axis, [(i, (i + 1) % count) for i in range(ends)]),
                cells,
                lax.ppermute(head, axis, [((i + 1) % count, i) for i in range(ends)]),
            ],
            axis=dim,
        )
    return cells


def from_behind(value, axis, by):
    count = lax.axis_size(axis)
    pairs = [(i, i + by) for i in range(count) if 0 <= i + by < count]
    return lax.ppermute(value, axis, pairs)


def head_normed(projected, gain):
    n_rows = projected.shape[0]
    heads = projected.reshape(n_rows, HEADS, HEAD)
    scaled = heads * lax.rsqrt(jnp.mean(heads * heads, axis=-1, keepdims=True) + epsilon)
    return (scaled * gain).reshape(n_rows, D).astype(jnp.bfloat16)


def keys_values(inputs, weight_k, weight_v, gain_k):
    keys = head_normed(jnp.dot(inputs, weight_k, preferred_element_type=jnp.float32), gain_k)
    values = jnp.dot(inputs, weight_v, preferred_element_type=jnp.float32).astype(jnp.bfloat16)
    return jnp.stack([keys, values])


def attend(queries, blocks, tile_index, usable):
    n_query = tile_index.shape[0]
    key_heads = jnp.take(blocks[0], tile_index, axis=0).reshape(n_query, -1, HEADS, HEAD)
    value_heads = jnp.take(blocks[1], tile_index, axis=0).reshape(n_query, -1, HEADS, HEAD)
    query_heads = queries.reshape(n_query, -1, HEADS, HEAD)
    scores = jnp.einsum(
        "pthe,pkhe->phtk", query_heads, key_heads, preferred_element_type=jnp.float32
    ) / math.sqrt(HEAD)
    listed = jnp.repeat(usable, TILE, axis=1).astype(jnp.float32)
    weights = jnp.exp(scores) * listed[:, None, None, :]
    totals = jnp.sum(weights, axis=-1)
    summed = jnp.einsum(
        "phtk,pkhe->pthe",
        weights.astype(jnp.bfloat16),
        value_heads,
        preferred_element_type=jnp.float32,
    )
    return summed / jnp.swapaxes(totals, 1, 2)[..., None]


def per_device(
    latent,
    stale_kv,
    query_weight,
    key_weight,
    value_weight,
    out_weight,
    query_gain,
    key_gain,
    tile_mask,
):
    tok_dev = latent.shape[0]
    patch_rows = tok_dev // PATCHES
    tiles_dev = tile_mask.shape[0]
    segment_id = lax.axis_index("segment")
    frame_id = lax.axis_index("seq")
    rounds = PATCHES + lax.axis_size("segment") - 1
    full_q, full_k, full_v, full_out = (
        lax.all_gather(query_weight[0], "seq", axis=0, tiled=True),
        lax.all_gather(key_weight[0], "seq", axis=0, tiled=True),
        lax.all_gather(value_weight[0], "seq", axis=0, tiled=True),
        lax.all_gather(out_weight[0], "seq", axis=0, tiled=True),
    )
    gain_q = query_gain[0]
    gain_k = key_gain[0]
    local_kv = stale_kv[0]
    window = extended(local_kv, (("seq", 1),), tok_dev)
    zero_rows = jnp.zeros((patch_rows, D), jnp.bfloat16)
    zero_pair = jnp.zeros((2, patch_rows, D), jnp.bfloat16)

    def project(inputs):
        fresh_q = head_normed(jnp.dot(inputs, full_q, preferred_element_type=jnp.float32), gain_q)
        return (fresh_q, keys_values(inputs, full_k, full_v, gain_k))

    def skip_project(inputs):
        return (zero_rows, zero_pair)

    def advance(round_id, carry):
        window, received, result = carry
        patch_id = round_id - segment_id
        active = (patch_id >= 0) & (patch_id < PATCHES)
        current = jnp.clip(patch_id, 0, PATCHES - 1)
        offset = current * patch_rows
        entering = lax.dynamic_slice_in_dim(latent, offset, patch_rows, 0)
        inputs = jnp.where(segment_id == 0, entering, received)
        fresh_q, own_kv = lax.cond(active, project, skip_project, inputs)
        spread = extended(own_kv, (("seq", 1),), patch_rows)
        trailing = spread[:, :patch_rows]
        leading = spread[:, 2 * patch_rows :]

        def finish(state):
            former, stored = state
            updated = lax.dynamic_update_slice_in_dim(former, trailing, offset, 1)
            updated = lax.dynamic_update_slice_in_dim(updated, own_kv, tok_dev + offset, 1)
            updated = lax.dynamic_update_slice_in_dim(updated, leading, 2 * tok_dev + offset, 1)
            listing = lax.dynamic_slice_in_dim(tile_mask, current * TPP, TPP, 0)
            usable = listing >= 0
            tile_index = jnp.where(usable, listing - (frame_id - 1) * tiles_dev, 0)
            blocks = updated.reshape(2, 3 * tiles_dev, TILE, D)
            attention = attend(fresh_q.reshape(TPP, TILE, D), blocks, tile_index, usable)
            attention_b = attention.reshape(patch_rows, D).astype(jnp.bfloat16)
            mixed = jnp.dot(attention_b, full_out, preferred_element_type=jnp.float32)
            leaving = (inputs.astype(jnp.float32) + mixed).astype(jnp.bfloat16)
            stored = lax.dynamic_update_slice_in_dim(stored, leaving, offset, 0)
            return (updated, stored, leaving)

        def remain(state):
            return (state[0], state[1], zero_rows)

        window, result, leaving = lax.cond(active, finish, remain, (window, result))
        received = from_behind(leaving, "segment", 1)
        return (window, received, result)

    initial = (window, zero_rows, jnp.zeros((tok_dev, D), jnp.bfloat16))
    final_state = lax.fori_loop(0, rounds, advance, initial)
    return final_state[2][None]


def solution(mesh):
    return jax.shard_map(
        per_device,
        mesh=mesh,
        in_specs=(
            P("seq", None),
            P("segment", None, "seq", None),
            P("segment", "seq", None),
            P("segment", "seq", None),
            P("segment", "seq", None),
            P("segment", "seq", None),
            P("segment", None),
            P("segment", None),
            P("seq", None),
        ),
        out_specs=P("segment", "seq", None),
        check_vma=False,
    )
```

profile of v0, /device:TPU:127, one launch (start us, length us, event | category | flops | bytes accessed | tf_op | source)
XLA Modules:
  0.0 1289.9 jit_solution(12764874456746758375)
XLA Ops:
  15.7 59.3 %collective-permute-done.3 = bf16[2,384,1536]{2,1,0:T(8,128)(2,1)S(1)} collective-permute-done((bf16[2,384,1536]{2,1,0:T(8,128)(2,1)}, bf16[2,384,1536]{2,1,0:T(8,128)(2,1)S(1)}, u32[]{:S(2)}, u32[]{:S(2)}) %collective-permute-start.3) | collective-permute-done | bytes 2359328 | tf_op jit(solution)/shard_map/ppermute | solution.py:24
  75.0 7.9 collective-permute-done.4
  82.9 5.7 pad_maximum_fusion.1
  88.6 15.1 %all-gather.9.cloned.1.call-done = bf16[1,1536,1536]{2,1,0:T(8,128)(2,1)} async-done(((bf16[1,48,1536]{2,1,0:T(8,128)(2,1)}), bf16[1,1536,1536]{2,1,0:T(8,128)(2,1)}) %all-gather.9.cloned.1.call-update) | async-done | bytes 4718608 | tf_op jit(solution)/shard_map/all_gather | solution.py:90
  103.7 81.8 %all-gather.11.cloned.1.call-done = bf16[1,1536,1536]{2,1,0:T(8,128)(2,1)} async-done(((bf16[1,48,1536]{2,1,0:T(8,128)(2,1)}), bf16[1,1536,1536]{2,1,0:T(8,128)(2,1)}) %all-gather.11.cloned.1.call-update) | async-done | bytes 4718608 | tf_op jit(solution)/shard_map/all_gather | solution.py:91
  185.4 83.4 %all-gather.13.cloned.1.call-done = bf16[1,1536,1536]{2,1,0:T(8,128)(2,1)} async-done(((bf16[1,48,1536]{2,1,0:T(8,128)(2,1)}), bf16[1,1536,1536]{2,1,0:T(8,128)(2,1)}) %all-gather.13.cloned.1.call-update) | async-done | bytes 4718608 | tf_op jit(solution)/shard_map/all_gather | solution.py:92
  268.9 83.3 %all-gather.15.cloned.1.call-done = bf16[1,1536,1536]{2,1,0:T(8,128)(2,1)} async-done(((bf16[1,48,1536]{2,1,0:T(8,128)(2,1)}), bf16[1,1536,1536]{2,1,0:T(8,128)(2,1)}) %all-gather.15.cloned.1.call-update) | async-done | bytes 4718608 | tf_op jit(solution)/shard_map/all_gather | solution.py:93
  353.3 930.1 %while.18 = (s32[]{:T(128)}, bf16[2,1152,1536]{2,1,0:T(8,128)(2,1)}, bf16[128,1536]{1,0:T(8,128)(2,1)S(1)}, bf16[384,1536]{1,0:T(8,128)(2,1)}, s32[]{:T(128)}, /...) while((s32[]{:T(128)}, ...), condition=%wide.region_8.10_spmd, body=%wide.region_0.9_spmd.sunk | while | flops 2727545344 | bytes 147957200 | solution.py:146
  360.9 11.2 collective-permute-done
  372.1 7.2 collective-permute-done.1
  381.4 6.9 collective-permute-done.2
  394.7 9.7 collective-permute-done
  404.4 5.2 collective-permute-done.1
  411.7 8.9 collective-permute-done.2
  427.2 8.6 collective-permute-done
  435.7 5.2 collective-permute-done.1
  443.0 10.0 collective-permute-done.2
  459.6 9.7 collective-permute-done
  469.2 5.2 collective-permute-done.1
  476.5 8.9 collective-permute-done.2
  492.0 9.7 collective-permute-done
  501.6 5.2 collective-permute-done.1
  508.9 8.9 collective-permute-done.2
  524.4 9.7 collective-permute-done
  534.0 5.2 collective-permute-done.1
  541.4 8.9 collective-permute-done.2
  556.8 7.4 collective-permute-done
  564.2 5.2 collective-permute-done.1
  571.5 419.4 %collective-permute-done.2 = bf16[128,1536]{1,0:T(8,128)(2,1)S(1)} collective-permute-done((bf16[128,1536]{1,0:T(8,128)(2,1)}, bf16[128,1536]{1,0:T(8,128)(2,1)S(1)}, u32[]{:S(2)}, u32[]{:S(2)}) %collective-permute-start.2) | collective-permute-done | bytes 393248 | tf_op jit(solution)/shard_map/while/body/eval_jaxpr/ppermute | solution.py:36
  992.1 9.9 conditional.4
  1007.3 7.4 collective-permute-done
  1014.7 5.2 collective-permute-done.1
  1020.0 54.0 %conditional.5 = (bf16[2,1152,1536]{2,1,0:T(8,128)(2,1)}, bf16[384,1536]{1,0:T(8,128)(2,1)}, bf16[128,1536]{1,0:T(8,128)(2,1)}) conditional(s32[]{:T(128)} %convert_element_type.58, (bf16[2,1152,1536]{2,1,0:T(8,128)(2,1)}, bf16[384,1536]{1,0:T(8,128)(2,1)}) %tuple.60, (s32[]{:T(128)}, bf16[2,1152,1536]{2,1,0:T(8,128)(2,1)}, ...), branch_computations={%region_5.5_spmd, %region_6.8_spmd} | conditional | flops 912850560 | bytes 86146920 | solution.py:141
  1033.6 5.3 fusion.25
  1051.5 5.5 reshape.55
  1075.3 14.0 %collective-permute-done.2 = bf16[128,1536]{1,0:T(8,128)(2,1)S(1)} collective-permute-done((bf16[128,1536]{1,0:T(8,128)(2,1)}, bf16[128,1536]{1,0:T(8,128)(2,1)S(1)}, u32[]{:S(2)}, u32[]{:S(2)}) %collective-permute-start.2) | collective-permute-done | bytes 393248 | tf_op jit(solution)/shard_map/while/body/eval_jaxpr/ppermute | solution.py:36
  1090.3 9.9 conditional.4
  1105.6 7.4 collective-permute-done
  1113.0 5.2 collective-permute-done.1
  1118.2 54.0 %conditional.5 = (bf16[2,1152,1536]{2,1,0:T(8,128)(2,1)}, bf16[384,1536]{1,0:T(8,128)(2,1)}, bf16[128,1536]{1,0:T(8,128)(2,1)}) conditional(s32[]{:T(128)} %convert_element_type.58, (bf16[2,1152,1536]{2,1,0:T(8,128)(2,1)}, bf16[384,1536]{1,0:T(8,128)(2,1)}) %tuple.60, (s32[]{:T(128)}, bf16[2,1152,1536]{2,1,0:T(8,128)(2,1)}, ...), branch_computations={%region_5.5_spmd, %region_6.8_spmd} | conditional | flops 912850560 | bytes 86146920 | solution.py:141
  1131.9 5.3 fusion.25
  1149.8 5.5 reshape.55
  1173.6 18.1 %collective-permute-done.2 = bf16[128,1536]{1,0:T(8,128)(2,1)S(1)} collective-permute-done((bf16[128,1536]{1,0:T(8,128)(2,1)}, bf16[128,1536]{1,0:T(8,128)(2,1)S(1)}, u32[]{:S(2)}, u32[]{:S(2)}) %collective-permute-start.2) | collective-permute-done | bytes 393248 | tf_op jit(solution)/shard_map/while/body/eval_jaxpr/ppermute | solution.py:36
  1192.7 9.9 conditional.4
  1208.0 12.8 collective-permute-done
  1225.7 53.8 %conditional.5 = (bf16[2,1152,1536]{2,1,0:T(8,128)(2,1)}, bf16[384,1536]{1,0:T(8,128)(2,1)}, bf16[128,1536]{1,0:T(8,128)(2,1)}) conditional(s32[]{:T(128)} %convert_element_type.58, (bf16[2,1152,1536]{2,1,0:T(8,128)(2,1)}, bf16[384,1536]{1,0:T(8,128)(2,1)}) %tuple.60, (s32[]{:T(128)}, bf16[2,1152,1536]{2,1,0:T(8,128)(2,1)}, ...), branch_computations={%region_5.5_spmd, %region_6.8_spmd} | conditional | flops 912850560 | bytes 86146920 | solution.py:141
  1239.2 5.3 fusion.25
  1257.1 5.5 reshape.55
  (244 shorter events, 266.1 us)
Async XLA Ops:
  6.5 97.1 %all-gather.9.cloned.1.call-start = ((), (), s32[]{:S(2)}) async-start(), calls=%async_computation | async-start | bytes 4866048 | tf_op jit(solution)/shard_map/all_gather | solution.py:90
  7.3 178.2 %all-gather.11.cloned.1.call-start = ((), (), s32[]{:S(2)}) async-start(), calls=%async_computation.1 | async-start | bytes 4866048 | tf_op jit(solution)/shard_map/all_gather | solution.py:91
  8.0 260.9 %all-gather.13.cloned.1.call-start = ((), (), s32[]{:S(2)}) async-start(), calls=%async_computation.2 | async-start | bytes 4866048 | tf_op jit(solution)/shard_map/all_gather | solution.py:92
  8.7 343.4 %all-gather.15.cloned.1.call-start = ((), (), s32[]{:S(2)}) async-start(), calls=%async_computation.3 | async-start | bytes 4866048 | tf_op jit(solution)/shard_map/all_gather | solution.py:93
  9.3 65.7 %collective-permute-start.3 = (bf16[2,384,1536]{2,1,0:T(8,128)(2,1)}, bf16[2,384,1536]{2,1,0:T(8,128)(2,1)S(1)}, u32[]{:S(2)}, u32[]{:S(2)}) collective-permute-start(bf16[2,384,1536]{2,1,0:T(8,128)(2,1)} %bitcast.66), channel_id=1, source_target_pairs={{0,1},{1,2},{2,3},{3,4},{4,5},{5,6},{6,7},{7,8},{8,9},{9,10},{10,1... | collective-permute-start | bytes 7077896 | tf_op jit(solution)/shard_map/ppermute | solution.py:24
  13.7 69.2 %collective-permute-start.4 = (bf16[2,384,1536]{2,1,0:T(8,128)(2,1)}, bf16[2,384,1536]{2,1,0:T(8,128)(2,1)}, u32[]{:S(2)}, u32[]{:S(2)}) collective-permute-start(bf16[2,384,1536]{2,1,0:T(8,128)(2,1)} %bitcast.67), channel_id=1, source_target_pairs={{1,0},{2,1},{3,2},{4,3},{5,4},{6,5},{7,6},{8,7},{9,8},{10,9},{11,1... | collective-permute-start | bytes 7077896 | tf_op jit(solution)/shard_map/ppermute | solution.py:26
  15.7 337.6 %copy-start.5 = (f32[1,128]{1,0:T(1,128)S(1)}, f32[1,128]{1,0:T(1,128)}, u32[]{:S(2)}) copy-start(f32[1,128]{1,0:T(1,128)} %param.23) | copy-start | bytes 1540
  354.5 17.6 %collective-permute-start = (bf16[2,128,1536]{2,1,0:T(8,128)(2,1)S(1)}, bf16[2,128,1536]{2,1,0:T(8,128)(2,1)S(1)}, u32[]{:S(2)}, u32[]{:S(2)}) collective-permute-start(bf16[2,128,1536]{2,1,0:T(8,128)(2,1)S(1)} %get-tuple-element.507), channel_id=1, source_target_pairs={{0,1},{1,2},{2,3},{3,4},{4,5},{5,6},{6,7},{7,8},{8,9},{9,10},{10,1... | collective-permute-start | bytes 2359304 | tf_op jit(solution)/shard_map/while/body/eval_jaxpr/ppermute | solution.py:24
  359.0 20.3 %collective-permute-start.1 = (bf16[2,128,1536]{2,1,0:T(8,128)(2,1)S(1)}, bf16[2,128,1536]{2,1,0:T(8,128)(2,1)S(1)}, u32[]{:S(2)}, u32[]{:S(2)}) collective-permute-start(bf16[2,128,1536]{2,1,0:T(8,128)(2,1)S(1)} %get-tuple-element.507), channel_id=1, source_target_pairs={{1,0},{2,1},{3,2},{4,3},{5,4},{6,5},{7,6},{8,7},{9,8},{10,9},{11,1... | collective-permute-start | bytes 2359304 | tf_op jit(solution)/shard_map/while/body/eval_jaxpr/ppermute | solution.py:26
  380.1 8.2 collective-permute-start.2
  389.4 14.9 %collective-permute-start = (bf16[2,128,1536]{2,1,0:T(8,128)(2,1)S(1)}, bf16[2,128,1536]{2,1,0:T(8,128)(2,1)S(1)}, u32[]{:S(2)}, u32[]{:S(2)}) collective-permute-start(bf16[2,128,1536]{2,1,0:T(8,128)(2,1)S(1)} %get-tuple-element.507), channel_id=1, source_target_pairs={{0,1},{1,2},{2,3},{3,4},{4,5},{5,6},{6,7},{7,8},{8,9},{9,10},{10,1... | collective-permute-start | bytes 2359304 | tf_op jit(solution)/shard_map/while/body/eval_jaxpr/ppermute | solution.py:24
  391.4 18.3 %collective-permute-start.1 = (bf16[2,128,1536]{2,1,0:T(8,128)(2,1)S(1)}, bf16[2,128,1536]{2,1,0:T(8,128)(2,1)S(1)}, u32[]{:S(2)}, u32[]{:S(2)}) collective-permute-start(bf16[2,128,1536]{2,1,0:T(8,128)(2,1)S(1)} %get-tuple-element.507), channel_id=1, source_target_pairs={{1,0},{2,1},{3,2},{4,3},{5,4},{6,5},{7,6},{8,7},{9,8},{10,9},{11,1... | collective-permute-start | bytes 2359304 | tf_op jit(solution)/shard_map/while/body/eval_jaxpr/ppermute | solution.py:26
  410.4 10.2 collective-permute-start.2
  421.9 13.9 %collective-permute-start = (bf16[2,128,1536]{2,1,0:T(8,128)(2,1)S(1)}, bf16[2,128,1536]{2,1,0:T(8,128)(2,1)S(1)}, u32[]{:S(2)}, u32[]{:S(2)}) collective-permute-start(bf16[2,128,1536]{2,1,0:T(8,128)(2,1)S(1)} %get-tuple-element.507), channel_id=1, source_target_pairs={{0,1},{1,2},{2,3},{3,4},{4,5},{5,6},{6,7},{7,8},{8,9},{9,10},{10,1... | collective-permute-start | bytes 2359304 | tf_op jit(solution)/shard_map/while/body/eval_jaxpr/ppermute | solution.py:24
  423.8 17.2 %collective-permute-start.1 = (bf16[2,128,1536]{2,1,0:T(8,128)(2,1)S(1)}, bf16[2,128,1536]{2,1,0:T(8,128)(2,1)S(1)}, u32[]{:S(2)}, u32[]{:S(2)}) collective-permute-start(bf16[2,128,1536]{2,1,0:T(8,128)(2,1)S(1)} %get-tuple-element.507), channel_id=1, source_target_pairs={{1,0},{2,1},{3,2},{4,3},{5,4},{6,5},{7,6},{8,7},{9,8},{10,9},{11,1... | collective-permute-start | bytes 2359304 | tf_op jit(solution)/shard_map/while/body/eval_jaxpr/ppermute | solution.py:26
  441.7 11.3 collective-permute-start.2
  454.3 14.9 %collective-permute-start = (bf16[2,128,1536]{2,1,0:T(8,128)(2,1)S(1)}, bf16[2,128,1536]{2,1,0:T(8,128)(2,1)S(1)}, u32[]{:S(2)}, u32[]{:S(2)}) collective-permute-start(bf16[2,128,1536]{2,1,0:T(8,128)(2,1)S(1)} %get-tuple-element.507), channel_id=1, source_target_pairs={{0,1},{1,2},{2,3},{3,4},{4,5},{5,6},{6,7},{7,8},{8,9},{9,10},{10,1... | collective-permute-start | bytes 2359304 | tf_op jit(solution)/shard_map/while/body/eval_jaxpr/ppermute | solution.py:24
  456.2 18.3 %collective-permute-start.1 = (bf16[2,128,1536]{2,1,0:T(8,128)(2,1)S(1)}, bf16[2,128,1536]{2,1,0:T(8,128)(2,1)S(1)}, u32[]{:S(2)}, u32[]{:S(2)}) collective-permute-start(bf16[2,128,1536]{2,1,0:T(8,128)(2,1)S(1)} %get-tuple-element.507), channel_id=1, source_target_pairs={{1,0},{2,1},{3,2},{4,3},{5,4},{6,5},{7,6},{8,7},{9,8},{10,9},{11,1... | collective-permute-start | bytes 2359304 | tf_op jit(solution)/shard_map/while/body/eval_jaxpr/ppermute | solution.py:26
  475.2 10.2 collective-permute-start.2
  486.7 14.9 %collective-permute-start = (bf16[2,128,1536]{2,1,0:T(8,128)(2,1)S(1)}, bf16[2,128,1536]{2,1,0:T(8,128)(2,1)S(1)}, u32[]{:S(2)}, u32[]{:S(2)}) collective-permute-start(bf16[2,128,1536]{2,1,0:T(8,128)(2,1)S(1)} %get-tuple-element.507), channel_id=1, source_target_pairs={{0,1},{1,2},{2,3},{3,4},{4,5},{5,6},{6,7},{7,8},{8,9},{9,10},{10,1... | collective-permute-start | bytes 2359304 | tf_op jit(solution)/shard_map/while/body/eval_jaxpr/ppermute | solution.py:24
  488.6 18.3 %collective-permute-start.1 = (bf16[2,128,1536]{2,1,0:T(8,128)(2,1)S(1)}, bf16[2,128,1536]{2,1,0:T(8,128)(2,1)S(1)}, u32[]{:S(2)}, u32[]{:S(2)}) collective-permute-start(bf16[2,128,1536]{2,1,0:T(8,128)(2,1)S(1)} %get-tuple-element.507), channel_id=1, source_target_pairs={{1,0},{2,1},{3,2},{4,3},{5,4},{6,5},{7,6},{8,7},{9,8},{10,9},{11,1... | collective-permute-start | bytes 2359304 | tf_op jit(solution)/shard_map/while/body/eval_jaxpr/ppermute | solution.py:26
  507.7 10.2 collective-permute-start.2
  519.1 14.9 %collective-permute-start = (bf16[2,128,1536]{2,1,0:T(8,128)(2,1)S(1)}, bf16[2,128,1536]{2,1,0:T(8,128)(2,1)S(1)}, u32[]{:S(2)}, u32[]{:S(2)}) collective-permute-start(bf16[2,128,1536]{2,1,0:T(8,128)(2,1)S(1)} %get-tuple-element.507), channel_id=1, source_target_pairs={{0,1},{1,2},{2,3},{3,4},{4,5},{5,6},{6,7},{7,8},{8,9},{9,10},{10,1... | collective-permute-start | bytes 2359304 | tf_op jit(solution)/shard_map/while/body/eval_jaxpr/ppermute | solution.py:24
  521.0 18.3 %collective-permute-start.1 = (bf16[2,128,1536]{2,1,0:T(8,128)(2,1)S(1)}, bf16[2,128,1536]{2,1,0:T(8,128)(2,1)S(1)}, u32[]{:S(2)}, u32[]{:S(2)}) collective-permute-start(bf16[2,128,1536]{2,1,0:T(8,128)(2,1)S(1)} %get-tuple-element.507), channel_id=1, source_target_pairs={{1,0},{2,1},{3,2},{4,3},{5,4},{6,5},{7,6},{8,7},{9,8},{10,9},{11,1... | collective-permute-start | bytes 2359304 | tf_op jit(solution)/shard_map/while/body/eval_jaxpr/ppermute | solution.py:26
  540.1 10.2 collective-permute-start.2
  551.5 12.7 collective-permute-start
  553.4 16.1 %collective-permute-start.1 = (bf16[2,128,1536]{2,1,0:T(8,128)(2,1)S(1)}, bf16[2,128,1536]{2,1,0:T(8,128)(2,1)S(1)}, u32[]{:S(2)}, u32[]{:S(2)}) collective-permute-start(bf16[2,128,1536]{2,1,0:T(8,128)(2,1)S(1)} %get-tuple-element.507), channel_id=1, source_target_pairs={{1,0},{2,1},{3,2},{4,3},{5,4},{6,5},{7,6},{8,7},{9,8},{10,9},{11,1... | collective-permute-start | bytes 2359304 | tf_op jit(solution)/shard_map/while/body/eval_jaxpr/ppermute | solution.py:26
  570.3 420.7 %collective-permute-start.2 = (bf16[128,1536]{1,0:T(8,128)(2,1)}, bf16[128,1536]{1,0:T(8,128)(2,1)S(1)}, u32[]{:S(2)}, u32[]{:S(2)}) collective-permute-start(bf16[128,1536]{1,0:T(8,128)(2,1)} %get-tuple-element.510), channel_id=1, source_target_pairs={{0,32},{32,64},{64,96},{96,128},{128,160},{160,192},{192,224},{1,3... | collective-permute-start | bytes 1179656 | tf_op jit(solution)/shard_map/while/body/eval_jaxpr/ppermute | solution.py:36
  1002.0 12.7 collective-permute-start
  1003.9 16.1 %collective-permute-start.1 = (bf16[2,128,1536]{2,1,0:T(8,128)(2,1)S(1)}, bf16[2,128,1536]{2,1,0:T(8,128)(2,1)S(1)}, u32[]{:S(2)}, u32[]{:S(2)}) collective-permute-start(bf16[2,128,1536]{2,1,0:T(8,128)(2,1)S(1)} %get-tuple-element.507), channel_id=1, source_target_pairs={{1,0},{2,1},{3,2},{4,3},{5,4},{6,5},{7,6},{8,7},{9,8},{10,9},{11,1... | collective-permute-start | bytes 2359304 | tf_op jit(solution)/shard_map/while/body/eval_jaxpr/ppermute | solution.py:26
  1020.0 9.1 copy-start
  1020.0 9.1 copy-start.3
  1051.5 5.6 copy-start.4
  1062.1 7.2 slice-start
  1074.0 15.3 %collective-permute-start.2 = (bf16[128,1536]{1,0:T(8,128)(2,1)}, bf16[128,1536]{1,0:T(8,128)(2,1)S(1)}, u32[]{:S(2)}, u32[]{:S(2)}) collective-permute-start(bf16[128,1536]{1,0:T(8,128)(2,1)} %get-tuple-element.510), channel_id=1, source_target_pairs={{0,32},{32,64},{64,96},{96,128},{128,160},{160,192},{192,224},{1,3... | collective-permute-start | bytes 1179656 | tf_op jit(solution)/shard_map/while/body/eval_jaxpr/ppermute | solution.py:36
  1100.3 12.7 collective-permute-start
  1102.2 16.1 %collective-permute-start.1 = (bf16[2,128,1536]{2,1,0:T(8,128)(2,1)S(1)}, bf16[2,128,1536]{2,1,0:T(8,128)(2,1)S(1)}, u32[]{:S(2)}, u32[]{:S(2)}) collective-permute-start(bf16[2,128,1536]{2,1,0:T(8,128)(2,1)S(1)} %get-tuple-element.507), channel_id=1, source_target_pairs={{1,0},{2,1},{3,2},{4,3},{5,4},{6,5},{7,6},{8,7},{9,8},{10,9},{11,1... | collective-permute-start | bytes 2359304 | tf_op jit(solution)/shard_map/while/body/eval_jaxpr/ppermute | solution.py:26
  1118.2 9.1 copy-start
  1118.3 9.1 copy-start.3
  1149.8 5.6 copy-start.4
  1160.4 7.2 slice-start
  1172.3 19.4 %collective-permute-start.2 = (bf16[128,1536]{1,0:T(8,128)(2,1)}, bf16[128,1536]{1,0:T(8,128)(2,1)S(1)}, u32[]{:S(2)}, u32[]{:S(2)}) collective-permute-start(bf16[128,1536]{1,0:T(8,128)(2,1)} %get-tuple-element.510), channel_id=1, source_target_pairs={{0,32},{32,64},{64,96},{96,128},{128,160},{160,192},{192,224},{1,3... | collective-permute-start | bytes 1179656 | tf_op jit(solution)/shard_map/while/body/eval_jaxpr/ppermute | solution.py:36
  1202.7 18.1 %collective-permute-start = (bf16[2,128,1536]{2,1,0:T(8,128)(2,1)S(1)}, bf16[2,128,1536]{2,1,0:T(8,128)(2,1)S(1)}, u32[]{:S(2)}, u32[]{:S(2)}) collective-permute-start(bf16[2,128,1536]{2,1,0:T(8,128)(2,1)S(1)} %get-tuple-element.507), channel_id=1, source_target_pairs={{0,1},{1,2},{2,3},{3,4},{4,5},{5,6},{6,7},{7,8},{8,9},{9,10},{10,1... | collective-permute-start | bytes 2359304 | tf_op jit(solution)/shard_map/while/body/eval_jaxpr/ppermute | solution.py:24
  1204.6 21.1 %collective-permute-start.1 = (bf16[2,128,1536]{2,1,0:T(8,128)(2,1)S(1)}, bf16[2,128,1536]{2,1,0:T(8,128)(2,1)S(1)}, u32[]{:S(2)}, u32[]{:S(2)}) collective-permute-start(bf16[2,128,1536]{2,1,0:T(8,128)(2,1)S(1)} %get-tuple-element.507), channel_id=1, source_target_pairs={{1,0},{2,1},{3,2},{4,3},{5,4},{6,5},{7,6},{8,7},{9,8},{10,9},{11,1... | collective-permute-start | bytes 2359304 | tf_op jit(solution)/shard_map/while/body/eval_jaxpr/ppermute | solution.py:26
  1225.7 9.1 copy-start
  1225.7 9.1 copy-start.3
  1267.8 7.2 slice-start
  1279.5 3.8 collective-permute-start.2
  (10 other events, 42.2 us)
Sparse Core Ops, SparseCore 0:
  9.9 93.6 all-gather.8
  106.3 79.1 all-gather.10
  188.0 80.7 all-gather.12
  271.3 80.7 all-gather.14
where the time goes:
time: 1290 us
  waiting for transfers between devices  988 us (77%)
  local copies, waits for them, and re-layouts  128 us (10%)
  starting transfers between devices  73.2 us (6%)
  matrix products  52.2 us (4%)
  other arithmetic  34.5 us (3%)
  between operations  13.2 us (1%)
    ppermute x10, waiting for transfers between devices, from_behind(): return lax.ppermute(value, axis, pairs)  507 us
    ppermute x11, waiting for transfers between devices, extended(): lax.ppermute(tail, axis, [(i, (i + 1) % count) for i in range(ends)])  153 us
    all_gather x1, waiting for transfers between devices, per_device(): lax.all_gather(value_weight[0], 'seq', axis=0, tiled=True)  83.4 us
    all_gather x1, waiting for transfers between devices, per_device(): lax.all_gather(out_weight[0], 'seq', axis=0, tiled=True)  83.3 us
    all_gather x1, waiting for transfers between devices, per_device(): lax.all_gather(key_weight[0], 'seq', axis=0, tiled=True)  81.8 us
    ppermute x11, waiting for transfers between devices, extended(): lax.ppermute(head, axis, [((i + 1) % count, i) for i in range(ends)])  62 us
    ppermute x11, starting transfers between devices, extended(): lax.ppermute(head, axis, [((i + 1) % count, i) for i in range(ends)])  34.1 us
    ppermute x11, starting transfers between devices, extended(): lax.ppermute(tail, axis, [(i, (i + 1) % count) for i in range(ends)])  26.1 us
  transfers between devices with their start and end apart: 36, of which 36 were waited for; matrix products, arithmetic and copies ran while one was open for 0% of the time, Pallas kernels for 0%

commit v1 on v0

--- a/solution.py
+++ b/solution.py
@@ -11,6 +11,11 @@
 PATCHES = 3
 TPP = 2
 epsilon = 1e-06
+
+
+def gather_from_all(shard, axis, dim):
+    copies = jnp.concatenate([shard] * lax.axis_size(axis), axis=dim)
+    return lax.all_to_all(copies, axis, dim, dim, tiled=True)
 
 
 def extended(cells, sides, width):
@@ -88,7 +93,7 @@
     rounds = PATCHES + lax.axis_size("segment") - 1
     full_q, full_k, full_v, full_out = (
         lax.all_gather(query_weight[0], "seq", axis=0, tiled=True),
-        lax.all_gather(key_weight[0], "seq", axis=0, tiled=True),
+        gather_from_all(key_weight[0], "seq", 0),
         lax.all_gather(value_weight[0], "seq", axis=0, tiled=True),
         lax.all_gather(out_weight[0], "seq", axis=0, tiled=True),
     )

time: 1290 us -> 1270 us (0.984)
  waiting for transfers between devices: 988 us -> 938 us
  local copies, waits for them, and re-layouts: 128 us -> 144 us
    ppermute x11, waiting for transfers between devices: 153 us -> 272 us  [extended(): lax.ppermute(tail, axis, [(i, (i + 1) % count) for i in range(ends)])]
    all_gather x1 -> x0, waiting for transfers between devices: 81.8 us -> none  [per_device(): lax.all_gather(key_weight[0], 'seq', axis=0, tiled=True)]
    all_gather x1, waiting for transfers between devices: 83.4 us -> 17 us  [per_device(): lax.all_gather(value_weight[0], 'seq', axis=0, tiled=True)]
    unnamed x2 -> x39, local copies, waits for them, and re-layouts: 0.01 us -> 16.3 us
    all_gather x1, waiting for transfers between devices: 15.1 us -> 0.01 us  [per_device(): lax.all_gather(query_weight[0], 'seq', axis=0, tiled=True)]
  transfers between devices with their start and end apart: 36 -> 36, of which waited for: 36 -> 34; matrix products, arithmetic and copies ran while one was open for 0% -> 2% of each run, Pallas kernels for 0% -> 0%
where the time goes in v1:
time: 1270 us
  waiting for transfers between devices  938 us (74%)
  local copies, waits for them, and re-layouts  144 us (11%)
  starting transfers between devices  82.7 us (7%)
  matrix products  52.4 us (4%)
  other arithmetic  34.6 us (3%)
  between operations  13.4 us (1%)
    ppermute x10, waiting for transfers between devices, from_behind(): return lax.ppermute(value, axis, pairs)  506 us
    ppermute x11, waiting for transfers between devices, extended(): lax.ppermute(tail, axis, [(i, (i + 1) % count) for i in range(ends)])  272 us
    all_gather x1, waiting for transfers between devices, per_device(): lax.all_gather(out_weight[0], 'seq', axis=0, tiled=True)  83.3 us
    ppermute x11, waiting for transfers between devices, extended(): lax.ppermute(head, axis, [((i + 1) % count, i) for i in range(ends)])  56.9 us
    ppermute x11, starting transfers between devices, extended(): lax.ppermute(head, axis, [((i + 1) % count, i) for i in range(ends)])  34.1 us
    ppermute x11, starting transfers between devices, extended(): lax.ppermute(tail, axis, [(i, (i + 1) % count) for i in range(ends)])  26 us
  transfers between devices with their start and end apart: 36, of which 34 were waited for; matrix products, arithmetic and copies ran while one was open for 2% of the time, Pallas kernels for 0%

profile of v1, /device:TPU:127, one launch (start us, length us, event | category | flops | bytes accessed | tf_op | source)
XLA Modules:
  0.0 1266.3 jit_solution(18237520273633556937)
XLA Ops:
  24.5 9.7 all-to-all-start
  41.2 178.7 %collective-permute-done.3 = bf16[2,384,1536]{2,1,0:T(8,128)(2,1)} collective-permute-done((bf16[2,384,1536]{2,1,0:T(8,128)(2,1)S(1)}, bf16[2,384,1536]{2,1,0:T(8,128)(2,1)}, u32[]{:S(2)}, u32[]{:S(2)}) %collective-permute-start.3) | collective-permute-done | bytes 2359328 | tf_op jit(solution)/shard_map/ppermute | solution.py:29
  222.7 5.7 pad_maximum_fusion.1
  228.5 17.0 %all-gather.9.cloned.1.call-done = bf16[1,1536,1536]{2,1,0:T(8,128)(2,1)} async-done(((bf16[1,48,1536]{2,1,0:T(8,128)(2,1)}), bf16[1,1536,1536]{2,1,0:T(8,128)(2,1)}) %all-gather.9.cloned.1.call-update) | async-done | bytes 4718608 | tf_op jit(solution)/shard_map/all_gather | solution.py:97
  245.5 83.3 %all-gather.11.cloned.1.call-done = bf16[1,1536,1536]{2,1,0:T(8,128)(2,1)} async-done(((bf16[1,48,1536]{2,1,0:T(8,128)(2,1)}), bf16[1,1536,1536]{2,1,0:T(8,128)(2,1)}) %all-gather.11.cloned.1.call-update) | async-done | bytes 4718608 | tf_op jit(solution)/shard_map/all_gather | solution.py:98
  330.0 929.8 %while.18 = (s32[]{:T(128)}, bf16[2,1152,1536]{2,1,0:T(8,128)(2,1)}, bf16[128,1536]{1,0:T(8,128)(2,1)S(1)}, bf16[384,1536]{1,0:T(8,128)(2,1)}, s32[]{:T(128)}, /...) while((s32[]{:T(128)}, ...), condition=%wide.region_8.10_spmd, body=%wide.region_0.9_spmd.sunk | while | flops 2727545344 | bytes 147957200 | solution.py:151
  337.6 11.2 collective-permute-done
  348.8 7.2 collective-permute-done.1
  358.1 6.9 collective-permute-done.2
  371.5 9.7 collective-permute-done
  381.1 5.2 collective-permute-done.1
  388.4 8.9 collective-permute-done.2
  403.9 8.6 collective-permute-done
  412.4 5.2 collective-permute-done.1
  419.7 10.0 collective-permute-done.2
  436.3 9.7 collective-permute-done
  445.9 5.2 collective-permute-done.1
  453.3 8.9 collective-permute-done.2
  468.7 9.7 collective-permute-done
  478.3 5.2 collective-permute-done.1
  485.7 8.9 collective-permute-done.2
  501.1 9.7 collective-permute-done
  510.8 5.2 collective-permute-done.1
  518.1 8.9 collective-permute-done.2
  533.5 7.4 collective-permute-done
  540.9 5.2 collective-permute-done.1
  548.3 418.8 %collective-permute-done.2 = bf16[128,1536]{1,0:T(8,128)(2,1)S(1)} collective-permute-done((bf16[128,1536]{1,0:T(8,128)(2,1)}, bf16[128,1536]{1,0:T(8,128)(2,1)S(1)}, u32[]{:S(2)}, u32[]{:S(2)}) %collective-permute-start.2) | collective-permute-done | bytes 393248 | tf_op jit(solution)/shard_map/while/body/eval_jaxpr/ppermute | solution.py:41
  968.2 9.8 conditional.4
  983.2 7.4 collective-permute-done
  990.7 5.2 collective-permute-done.1
  995.9 54.0 %conditional.5 = (bf16[2,1152,1536]{2,1,0:T(8,128)(2,1)}, bf16[384,1536]{1,0:T(8,128)(2,1)}, bf16[128,1536]{1,0:T(8,128)(2,1)}) conditional(s32[]{:T(128)} %convert_element_type.58, (bf16[2,1152,1536]{2,1,0:T(8,128)(2,1)}, bf16[384,1536]{1,0:T(8,128)(2,1)}) %tuple.60, (s32[]{:T(128)}, bf16[2,1152,1536]{2,1,0:T(8,128)(2,1)}, ...), branch_computations={%region_5.5_spmd, %region_6.8_spmd} | conditional | flops 912850560 | bytes 86146920 | solution.py:146
  1009.5 5.4 fusion.25
  1027.5 5.5 reshape.57
  1051.2 13.9 %collective-permute-done.2 = bf16[128,1536]{1,0:T(8,128)(2,1)S(1)} collective-permute-done((bf16[128,1536]{1,0:T(8,128)(2,1)}, bf16[128,1536]{1,0:T(8,128)(2,1)S(1)}, u32[]{:S(2)}, u32[]{:S(2)}) %collective-permute-start.2) | collective-permute-done | bytes 393248 | tf_op jit(solution)/shard_map/while/body/eval_jaxpr/ppermute | solution.py:41
  1066.2 9.8 conditional.4
  1081.3 7.4 collective-permute-done
  1088.7 5.2 collective-permute-done.1
  1093.9 54.1 %conditional.5 = (bf16[2,1152,1536]{2,1,0:T(8,128)(2,1)}, bf16[384,1536]{1,0:T(8,128)(2,1)}, bf16[128,1536]{1,0:T(8,128)(2,1)}) conditional(s32[]{:T(128)} %convert_element_type.58, (bf16[2,1152,1536]{2,1,0:T(8,128)(2,1)}, bf16[384,1536]{1,0:T(8,128)(2,1)}) %tuple.60, (s32[]{:T(128)}, bf16[2,1152,1536]{2,1,0:T(8,128)(2,1)}, ...), branch_computations={%region_5.5_spmd, %region_6.8_spmd} | conditional | flops 912850560 | bytes 86146920 | solution.py:146
  1107.6 5.4 fusion.25
  1125.6 5.5 reshape.57
  1149.3 18.7 %collective-permute-done.2 = bf16[128,1536]{1,0:T(8,128)(2,1)S(1)} collective-permute-done((bf16[128,1536]{1,0:T(8,128)(2,1)}, bf16[128,1536]{1,0:T(8,128)(2,1)S(1)}, u32[]{:S(2)}, u32[]{:S(2)}) %collective-permute-start.2) | collective-permute-done | bytes 393248 | tf_op jit(solution)/shard_map/while/body/eval_jaxpr/ppermute | solution.py:41
  1169.1 9.8 conditional.4
  1184.2 12.9 %collective-permute-done = bf16[2,128,1536]{2,1,0:T(8,128)(2,1)S(1)} collective-permute-done((bf16[2,128,1536]{2,1,0:T(8,128)(2,1)S(1)}, bf16[2,128,1536]{2,1,0:T(8,128)(2,1)S(1)}, u32[]{:S(2)}, u32[]{:S(2)}) %collective-permute-start) | collective-permute-done | bytes 786464 | tf_op jit(solution)/shard_map/while/body/eval_jaxpr/ppermute | solution.py:29
  1197.1 5.0 collective-permute-done.1
  1202.1 53.9 %conditional.5 = (bf16[2,1152,1536]{2,1,0:T(8,128)(2,1)}, bf16[384,1536]{1,0:T(8,128)(2,1)}, bf16[128,1536]{1,0:T(8,128)(2,1)}) conditional(s32[]{:T(128)} %convert_element_type.58, (bf16[2,1152,1536]{2,1,0:T(8,128)(2,1)}, bf16[384,1536]{1,0:T(8,128)(2,1)}) %tuple.60, (s32[]{:T(128)}, bf16[2,1152,1536]{2,1,0:T(8,128)(2,1)}, ...), branch_computations={%region_5.5_spmd, %region_6.8_spmd} | conditional | flops 912850560 | bytes 86146920 | solution.py:146
  1215.6 5.4 fusion.25
  1233.6 5.5 reshape.57
  1239.5 4.7 bitcast_reduce_fusion
  (281 shorter events, 274.5 us)
Async XLA Ops:
  6.5 15.4 %copy-start.2 = (bf16[1,48,1536]{2,1,0:T(8,128)(2,1)S(1)}, bf16[1,48,1536]{2,1,0:T(8,128)(2,1)}, u32[]{:S(2)}) copy-start(bf16[1,48,1536]{2,1,0:T(8,128)(2,1)} %param.20) | copy-start | bytes 442372
  6.5 221.9 %all-gather.7.cloned.1.call-start = ((), (), s32[]{:S(2)}) async-start(), calls=%async_computation.1 | async-start | bytes 4866048 | tf_op jit(solution)/shard_map/all_gather | solution.py:95
  7.3 238.2 %all-gather.9.cloned.1.call-start = ((), (), s32[]{:S(2)}) async-start(), calls=%async_computation.2 | async-start | bytes 4866048 | tf_op jit(solution)/shard_map/all_gather | solution.py:97
  24.5 10.5 copy-start.7
  24.5 204.0 %all-to-all-start = ((bf16[32,48,1536]{2,1,0:T(8,128)(2,1)}), bf16[32,48,1536]{2,1,0:T(8,128)(2,1)}, u32[]{:S(2)}, u32[]{:S(2)}) async-start(bf16[32,48,1536]{2,1,0:T(8,128)(2,1)} %bitcast.99), calls=%async_computation | async-start | bytes 9437184 | tf_op jit(solution)/shard_map/all_to_all | solution.py:18
  34.2 294.6 %all-gather.11.cloned.1.call-start = ((), (), s32[]{:S(2)}) async-start(), calls=%async_computation.3 | async-start | bytes 4866048 | tf_op jit(solution)/shard_map/all_gather | solution.py:98
  35.0 184.9 %collective-permute-start.3 = (bf16[2,384,1536]{2,1,0:T(8,128)(2,1)S(1)}, bf16[2,384,1536]{2,1,0:T(8,128)(2,1)}, u32[]{:S(2)}, u32[]{:S(2)}) collective-permute-start(bf16[2,384,1536]{2,1,0:T(8,128)(2,1)S(1)} %bitcast.100), channel_id=1, source_target_pairs={{0,1},{1,2},{2,3},{3,4},{4,5},{5,6},{6,7},{7,8},{8,9},{9,10},{10,1... | collective-permute-start | bytes 7077896 | tf_op jit(solution)/shard_map/ppermute | solution.py:29
  39.3 183.4 %collective-permute-start.4 = (bf16[2,384,1536]{2,1,0:T(8,128)(2,1)S(1)}, bf16[2,384,1536]{2,1,0:T(8,128)(2,1)}, u32[]{:S(2)}, u32[]{:S(2)}) collective-permute-start(bf16[2,384,1536]{2,1,0:T(8,128)(2,1)S(1)} %bitcast.101), channel_id=1, source_target_pairs={{1,0},{2,1},{3,2},{4,3},{5,4},{6,5},{7,6},{8,7},{9,8},{10,9},{11,1... | collective-permute-start | bytes 7077896 | tf_op jit(solution)/shard_map/ppermute | solution.py:31
  41.2 288.7 %copy-start.8 = (f32[1,128]{1,0:T(1,128)S(1)}, f32[1,128]{1,0:T(1,128)}, u32[]{:S(2)}) copy-start(f32[1,128]{1,0:T(1,128)} %param.23) | copy-start | bytes 1540
  331.2 17.6 %collective-permute-start = (bf16[2,128,1536]{2,1,0:T(8,128)(2,1)S(1)}, bf16[2,128,1536]{2,1,0:T(8,128)(2,1)S(1)}, u32[]{:S(2)}, u32[]{:S(2)}) collective-permute-start(bf16[2,128,1536]{2,1,0:T(8,128)(2,1)S(1)} %get-tuple-element.507), channel_id=1, source_target_pairs={{0,1},{1,2},{2,3},{3,4},{4,5},{5,6},{6,7},{7,8},{8,9},{9,10},{10,1... | collective-permute-start | bytes 2359304 | tf_op jit(solution)/shard_map/while/body/eval_jaxpr/ppermute | solution.py:29
  335.7 20.3 %collective-permute-start.1 = (bf16[2,128,1536]{2,1,0:T(8,128)(2,1)S(1)}, bf16[2,128,1536]{2,1,0:T(8,128)(2,1)S(1)}, u32[]{:S(2)}, u32[]{:S(2)}) collective-permute-start(bf16[2,128,1536]{2,1,0:T(8,128)(2,1)S(1)} %get-tuple-element.507), channel_id=1, source_target_pairs={{1,0},{2,1},{3,2},{4,3},{5,4},{6,5},{7,6},{8,7},{9,8},{10,9},{11,1... | collective-permute-start | bytes 2359304 | tf_op jit(solution)/shard_map/while/body/eval_jaxpr/ppermute | solution.py:31
  356.8 8.2 collective-permute-start.2
  366.2 14.9 %collective-permute-start = (bf16[2,128,1536]{2,1,0:T(8,128)(2,1)S(1)}, bf16[2,128,1536]{2,1,0:T(8,128)(2,1)S(1)}, u32[]{:S(2)}, u32[]{:S(2)}) collective-permute-start(bf16[2,128,1536]{2,1,0:T(8,128)(2,1)S(1)} %get-tuple-element.507), channel_id=1, source_target_pairs={{0,1},{1,2},{2,3},{3,4},{4,5},{5,6},{6,7},{7,8},{8,9},{9,10},{10,1... | collective-permute-start | bytes 2359304 | tf_op jit(solution)/shard_map/while/body/eval_jaxpr/ppermute | solution.py:29
  368.1 18.3 %collective-permute-start.1 = (bf16[2,128,1536]{2,1,0:T(8,128)(2,1)S(1)}, bf16[2,128,1536]{2,1,0:T(8,128)(2,1)S(1)}, u32[]{:S(2)}, u32[]{:S(2)}) collective-permute-start(bf16[2,128,1536]{2,1,0:T(8,128)(2,1)S(1)} %get-tuple-element.507), channel_id=1, source_target_pairs={{1,0},{2,1},{3,2},{4,3},{5,4},{6,5},{7,6},{8,7},{9,8},{10,9},{11,1... | collective-permute-start | bytes 2359304 | tf_op jit(solution)/shard_map/while/body/eval_jaxpr/ppermute | solution.py:31
  387.1 10.2 collective-permute-start.2
  398.6 13.9 %collective-permute-start = (bf16[2,128,1536]{2,1,0:T(8,128)(2,1)S(1)}, bf16[2,128,1536]{2,1,0:T(8,128)(2,1)S(1)}, u32[]{:S(2)}, u32[]{:S(2)}) collective-permute-start(bf16[2,128,1536]{2,1,0:T(8,128)(2,1)S(1)} %get-tuple-element.507), channel_id=1, source_target_pairs={{0,1},{1,2},{2,3},{3,4},{4,5},{5,6},{6,7},{7,8},{8,9},{9,10},{10,1... | collective-permute-start | bytes 2359304 | tf_op jit(solution)/shard_map/while/body/eval_jaxpr/ppermute | solution.py:29
  400.5 17.2 %collective-permute-start.1 = (bf16[2,128,1536]{2,1,0:T(8,128)(2,1)S(1)}, bf16[2,128,1536]{2,1,0:T(8,128)(2,1)S(1)}, u32[]{:S(2)}, u32[]{:S(2)}) collective-permute-start(bf16[2,128,1536]{2,1,0:T(8,128)(2,1)S(1)} %get-tuple-element.507), channel_id=1, source_target_pairs={{1,0},{2,1},{3,2},{4,3},{5,4},{6,5},{7,6},{8,7},{9,8},{10,9},{11,1... | collective-permute-start | bytes 2359304 | tf_op jit(solution)/shard_map/while/body/eval_jaxpr/ppermute | solution.py:31
  418.5 11.3 collective-permute-start.2
  431.0 14.9 %collective-permute-start = (bf16[2,128,1536]{2,1,0:T(8,128)(2,1)S(1)}, bf16[2,128,1536]{2,1,0:T(8,128)(2,1)S(1)}, u32[]{:S(2)}, u32[]{:S(2)}) collective-permute-start(bf16[2,128,1536]{2,1,0:T(8,128)(2,1)S(1)} %get-tuple-element.507), channel_id=1, source_target_pairs={{0,1},{1,2},{2,3},{3,4},{4,5},{5,6},{6,7},{7,8},{8,9},{9,10},{10,1... | collective-permute-start | bytes 2359304 | tf_op jit(solution)/shard_map/while/body/eval_jaxpr/ppermute | solution.py:29
  432.9 18.3 %collective-permute-start.1 = (bf16[2,128,1536]{2,1,0:T(8,128)(2,1)S(1)}, bf16[2,128,1536]{2,1,0:T(8,128)(2,1)S(1)}, u32[]{:S(2)}, u32[]{:S(2)}) collective-permute-start(bf16[2,128,1536]{2,1,0:T(8,128)(2,1)S(1)} %get-tuple-element.507), channel_id=1, source_target_pairs={{1,0},{2,1},{3,2},{4,3},{5,4},{6,5},{7,6},{8,7},{9,8},{10,9},{11,1... | collective-permute-start | bytes 2359304 | tf_op jit(solution)/shard_map/while/body/eval_jaxpr/ppermute | solution.py:31
  452.0 10.2 collective-permute-start.2
  463.4 14.9 %collective-permute-start = (bf16[2,128,1536]{2,1,0:T(8,128)(2,1)S(1)}, bf16[2,128,1536]{2,1,0:T(8,128)(2,1)S(1)}, u32[]{:S(2)}, u32[]{:S(2)}) collective-permute-start(bf16[2,128,1536]{2,1,0:T(8,128)(2,1)S(1)} %get-tuple-element.507), channel_id=1, source_target_pairs={{0,1},{1,2},{2,3},{3,4},{4,5},{5,6},{6,7},{7,8},{8,9},{9,10},{10,1... | collective-permute-start | bytes 2359304 | tf_op jit(solution)/shard_map/while/body/eval_jaxpr/ppermute | solution.py:29
  465.3 18.3 %collective-permute-start.1 = (bf16[2,128,1536]{2,1,0:T(8,128)(2,1)S(1)}, bf16[2,128,1536]{2,1,0:T(8,128)(2,1)S(1)}, u32[]{:S(2)}, u32[]{:S(2)}) collective-permute-start(bf16[2,128,1536]{2,1,0:T(8,128)(2,1)S(1)} %get-tuple-element.507), channel_id=1, source_target_pairs={{1,0},{2,1},{3,2},{4,3},{5,4},{6,5},{7,6},{8,7},{9,8},{10,9},{11,1... | collective-permute-start | bytes 2359304 | tf_op jit(solution)/shard_map/while/body/eval_jaxpr/ppermute | solution.py:31
  484.4 10.2 collective-permute-start.2
  495.8 14.9 %collective-permute-start = (bf16[2,128,1536]{2,1,0:T(8,128)(2,1)S(1)}, bf16[2,128,1536]{2,1,0:T(8,128)(2,1)S(1)}, u32[]{:S(2)}, u32[]{:S(2)}) collective-permute-start(bf16[2,128,1536]{2,1,0:T(8,128)(2,1)S(1)} %get-tuple-element.507), channel_id=1, source_target_pairs={{0,1},{1,2},{2,3},{3,4},{4,5},{5,6},{6,7},{7,8},{8,9},{9,10},{10,1... | collective-permute-start | bytes 2359304 | tf_op jit(solution)/shard_map/while/body/eval_jaxpr/ppermute | solution.py:29
  497.7 18.3 %collective-permute-start.1 = (bf16[2,128,1536]{2,1,0:T(8,128)(2,1)S(1)}, bf16[2,128,1536]{2,1,0:T(8,128)(2,1)S(1)}, u32[]{:S(2)}, u32[]{:S(2)}) collective-permute-start(bf16[2,128,1536]{2,1,0:T(8,128)(2,1)S(1)} %get-tuple-element.507), channel_id=1, source_target_pairs={{1,0},{2,1},{3,2},{4,3},{5,4},{6,5},{7,6},{8,7},{9,8},{10,9},{11,1... | collective-permute-start | bytes 2359304 | tf_op jit(solution)/shard_map/while/body/eval_jaxpr/ppermute | solution.py:31
  516.8 10.2 collective-permute-start.2
  528.2 12.7 %collective-permute-start = (bf16[2,128,1536]{2,1,0:T(8,128)(2,1)S(1)}, bf16[2,128,1536]{2,1,0:T(8,128)(2,1)S(1)}, u32[]{:S(2)}, u32[]{:S(2)}) collective-permute-start(bf16[2,128,1536]{2,1,0:T(8,128)(2,1)S(1)} %get-tuple-element.507), channel_id=1, source_target_pairs={{0,1},{1,2},{2,3},{3,4},{4,5},{5,6},{6,7},{7,8},{8,9},{9,10},{10,1... | collective-permute-start | bytes 2359304 | tf_op jit(solution)/shard_map/while/body/eval_jaxpr/ppermute | solution.py:29
  530.1 16.1 %collective-permute-start.1 = (bf16[2,128,1536]{2,1,0:T(8,128)(2,1)S(1)}, bf16[2,128,1536]{2,1,0:T(8,128)(2,1)S(1)}, u32[]{:S(2)}, u32[]{:S(2)}) collective-permute-start(bf16[2,128,1536]{2,1,0:T(8,128)(2,1)S(1)} %get-tuple-element.507), channel_id=1, source_target_pairs={{1,0},{2,1},{3,2},{4,3},{5,4},{6,5},{7,6},{8,7},{9,8},{10,9},{11,1... | collective-permute-start | bytes 2359304 | tf_op jit(solution)/shard_map/while/body/eval_jaxpr/ppermute | solution.py:31
  547.0 420.1 %collective-permute-start.2 = (bf16[128,1536]{1,0:T(8,128)(2,1)}, bf16[128,1536]{1,0:T(8,128)(2,1)S(1)}, u32[]{:S(2)}, u32[]{:S(2)}) collective-permute-start(bf16[128,1536]{1,0:T(8,128)(2,1)} %get-tuple-element.510), channel_id=1, source_target_pairs={{0,32},{32,64},{64,96},{96,128},{128,160},{160,192},{192,224},{1,3... | collective-permute-start | bytes 1179656 | tf_op jit(solution)/shard_map/while/body/eval_jaxpr/ppermute | solution.py:41
  977.9 12.7 %collective-permute-start = (bf16[2,128,1536]{2,1,0:T(8,128)(2,1)S(1)}, bf16[2,128,1536]{2,1,0:T(8,128)(2,1)S(1)}, u32[]{:S(2)}, u32[]{:S(2)}) collective-permute-start(bf16[2,128,1536]{2,1,0:T(8,128)(2,1)S(1)} %get-tuple-element.507), channel_id=1, source_target_pairs={{0,1},{1,2},{2,3},{3,4},{4,5},{5,6},{6,7},{7,8},{8,9},{9,10},{10,1... | collective-permute-start | bytes 2359304 | tf_op jit(solution)/shard_map/while/body/eval_jaxpr/ppermute | solution.py:29
  979.8 16.1 %collective-permute-start.1 = (bf16[2,128,1536]{2,1,0:T(8,128)(2,1)S(1)}, bf16[2,128,1536]{2,1,0:T(8,128)(2,1)S(1)}, u32[]{:S(2)}, u32[]{:S(2)}) collective-permute-start(bf16[2,128,1536]{2,1,0:T(8,128)(2,1)S(1)} %get-tuple-element.507), channel_id=1, source_target_pairs={{1,0},{2,1},{3,2},{4,3},{5,4},{6,5},{7,6},{8,7},{9,8},{10,9},{11,1... | collective-permute-start | bytes 2359304 | tf_op jit(solution)/shard_map/while/body/eval_jaxpr/ppermute | solution.py:31
  995.9 9.1 copy-start
  995.9 9.1 copy-start.4
  1038.1 7.2 slice-start
  1049.9 15.2 %collective-permute-start.2 = (bf16[128,1536]{1,0:T(8,128)(2,1)}, bf16[128,1536]{1,0:T(8,128)(2,1)S(1)}, u32[]{:S(2)}, u32[]{:S(2)}) collective-permute-start(bf16[128,1536]{1,0:T(8,128)(2,1)} %get-tuple-element.510), channel_id=1, source_target_pairs={{0,32},{32,64},{64,96},{96,128},{128,160},{160,192},{192,224},{1,3... | collective-permute-start | bytes 1179656 | tf_op jit(solution)/shard_map/while/body/eval_jaxpr/ppermute | solution.py:41
  1076.0 12.7 %collective-permute-start = (bf16[2,128,1536]{2,1,0:T(8,128)(2,1)S(1)}, bf16[2,128,1536]{2,1,0:T(8,128)(2,1)S(1)}, u32[]{:S(2)}, u32[]{:S(2)}) collective-permute-start(bf16[2,128,1536]{2,1,0:T(8,128)(2,1)S(1)} %get-tuple-element.507), channel_id=1, source_target_pairs={{0,1},{1,2},{2,3},{3,4},{4,5},{5,6},{6,7},{7,8},{8,9},{9,10},{10,1... | collective-permute-start | bytes 2359304 | tf_op jit(solution)/shard_map/while/body/eval_jaxpr/ppermute | solution.py:29
  1077.9 16.1 %collective-permute-start.1 = (bf16[2,128,1536]{2,1,0:T(8,128)(2,1)S(1)}, bf16[2,128,1536]{2,1,0:T(8,128)(2,1)S(1)}, u32[]{:S(2)}, u32[]{:S(2)}) collective-permute-start(bf16[2,128,1536]{2,1,0:T(8,128)(2,1)S(1)} %get-tuple-element.507), channel_id=1, source_target_pairs={{1,0},{2,1},{3,2},{4,3},{5,4},{6,5},{7,6},{8,7},{9,8},{10,9},{11,1... | collective-permute-start | bytes 2359304 | tf_op jit(solution)/shard_map/while/body/eval_jaxpr/ppermute | solution.py:31
  1094.0 9.1 copy-start
  1094.0 9.1 copy-start.4
  1136.2 7.2 slice-start
  1148.0 20.0 %collective-permute-start.2 = (bf16[128,1536]{1,0:T(8,128)(2,1)}, bf16[128,1536]{1,0:T(8,128)(2,1)S(1)}, u32[]{:S(2)}, u32[]{:S(2)}) collective-permute-start(bf16[128,1536]{1,0:T(8,128)(2,1)} %get-tuple-element.510), channel_id=1, source_target_pairs={{0,32},{32,64},{64,96},{96,128},{128,160},{160,192},{192,224},{1,3... | collective-permute-start | bytes 1179656 | tf_op jit(solution)/shard_map/while/body/eval_jaxpr/ppermute | solution.py:41
  1178.9 18.2 %collective-permute-start = (bf16[2,128,1536]{2,1,0:T(8,128)(2,1)S(1)}, bf16[2,128,1536]{2,1,0:T(8,128)(2,1)S(1)}, u32[]{:S(2)}, u32[]{:S(2)}) collective-permute-start(bf16[2,128,1536]{2,1,0:T(8,128)(2,1)S(1)} %get-tuple-element.507), channel_id=1, source_target_pairs={{0,1},{1,2},{2,3},{3,4},{4,5},{5,6},{6,7},{7,8},{8,9},{9,10},{10,1... | collective-permute-start | bytes 2359304 | tf_op jit(solution)/shard_map/while/body/eval_jaxpr/ppermute | solution.py:29
  1180.8 21.3 %collective-permute-start.1 = (bf16[2,128,1536]{2,1,0:T(8,128)(2,1)S(1)}, bf16[2,128,1536]{2,1,0:T(8,128)(2,1)S(1)}, u32[]{:S(2)}, u32[]{:S(2)}) collective-permute-start(bf16[2,128,1536]{2,1,0:T(8,128)(2,1)S(1)} %get-tuple-element.507), channel_id=1, source_target_pairs={{1,0},{2,1},{3,2},{4,3},{5,4},{6,5},{7,6},{8,7},{9,8},{10,9},{11,1... | collective-permute-start | bytes 2359304 | tf_op jit(solution)/shard_map/while/body/eval_jaxpr/ppermute | solution.py:31
  1202.1 9.1 copy-start
  1202.1 9.1 copy-start.4
  1244.3 7.2 slice-start
  1256.0 3.8 collective-permute-start.2
  (13 other events, 57.5 us)
Sparse Core Ops, SparseCore 0:
  9.9 143.8 all-gather.6
  156.4 89.0 all-gather.8
  248.1 80.7 all-gather.10
